TPU v7x, 32 devices: a whole 2x2x4 slice. The times are simulated.
32 devices in a mesh: shot: 2 (over y), box: 8 (over z, x), sub: 2 (over core).
Axes of the slice: x: 2, y: 2, z: 4, core: 2. Of those that a mesh axis runs over, the one named last changes fastest.
Arguments:
- box_weights: float32 [64, 256, 128], P(('shot', 'box', 'sub')), parts along dimension 0, may hold values from -6 to 6
- velocity: float32 [8192], P('shot'), parts along dimension 0, may hold values from -4 to 4
- switch_kernel: float32 [128, 128], replicated, may hold values from -0.5 to 0.5
Outputs:
- final_weights: float32 [4, 4096, 128], P('shot', ('box', 'sub')), parts along dimension 0
There are 2 independent parts, one for each index of `shot`. A program takes and returns all parts, laid end to end along the dimension named above; an argument that names none is the same for every part. Nothing has to cross between parts.
All inputs are finite; a program needn't handle non-finite values.
Results may differ from a plain program's by a relative error of at most 0.00013.
Values sent between devices are 32-bit elements; how exact they have to be, the bound alone decides.
No kernel may reach another device: no remote copies, remote signals or barrier semaphores. Data moves between devices by JAX's collectives and lax.ppermute only.
A program may use at most 64 MiB of HBM per device.

v0:
```python
import jax
import jax.numpy as jnp
from jax import lax
from jax.sharding import PartitionSpec as P

CHEB = 8
half_root = 0.7071067811865476


def swapped(value, axis, apart):
    mask = 2**apart
    pairs = [(source, source ^ mask) for source in range(lax.axis_size(axis))]
    return lax.ppermute(value, axis, pairs)


def cheb_nodes():
    counter = jnp.arange(CHEB, dtype=jnp.float32)
    return jnp.cos(jnp.pi * (2.0 * counter + 1.0) / (2.0 * CHEB))


def lagrange_rows(points, node_values):
    differences = points[:, None] - node_values[None, :]
    node_gaps = node_values[:, None] - node_values[None, :]
    identity = jnp.eye(CHEB, dtype=jnp.float32)
    numerator = jnp.prod(
        jnp.where(identity[None, :, :] > 0.5, 1.0, differences[:, None, :]), axis=2
    )
    denominator = jnp.prod(jnp.where(identity > 0.5, 1.0, node_gaps), axis=1)
    return numerator / denominator[None, :]


def spread_coord(values, axis_dim):
    if axis_dim == 0:
        return jnp.repeat(values, CHEB)
    return jnp.tile(values, CHEB)


def level_tables(axis_dim):
    node_values = cheb_nodes()
    identity = jnp.eye(CHEB, dtype=jnp.float32)
    pair_eye = jnp.eye(2, dtype=jnp.float32)
    matrices = []
    coords = []
    for child_idx in (0, 1):
        child_pts = (node_values + (2.0 * child_idx - 1.0)) * 0.5
        lagrange = lagrange_rows(child_pts, node_values)
        if axis_dim == 0:
            single = jnp.kron(lagrange, identity)
        else:
            single = jnp.kron(identity, lagrange)
        matrices.append(jnp.kron(pair_eye, single))
        coords.append(spread_coord(child_pts, axis_dim))
    return (jnp.concatenate(matrices, 0), jnp.stack(coords), spread_coord(node_values, axis_dim))


def rotate(values, angles):
    real_part = values[..., : CHEB * CHEB]
    imag_part = values[..., CHEB * CHEB :]
    cosines = jnp.cos(angles)
    sine_vals = jnp.sin(angles)
    return jnp.concatenate(
        [real_part * cosines - imag_part * sine_vals, real_part * sine_vals + imag_part * cosines],
        -1,
    )


def merge_blocks(blocks, omegas, weights, coord_in, coord_out):
    phase = omegas[None, None, :, :, None]
    first_term = rotate(blocks[:, 0][:, :, None], -phase * coord_in[0])
    second_term = rotate(blocks[:, 1][:, :, None], -phase * coord_in[1])
    joined = jnp.concatenate([first_term, second_term], -1)
    mixture = jnp.dot(
        joined.reshape(-1, 4 * CHEB * CHEB),
        weights,
        precision=lax.Precision.HIGHEST,
        preferred_element_type=jnp.float32,
    )
    mixture = mixture.reshape(first_term.shape)
    return rotate(mixture, phase * coord_out) * half_root


def apply_switch(current, switch_kernel):
    flat = jnp.dot(
        current.reshape(-1, current.shape[-1]),
        switch_kernel,
        precision=lax.Precision.HIGHEST,
        preferred_element_type=jnp.float32,
    )
    return flat.reshape(current.shape)


def level_omegas(velocity, device, level_idx, tgt_count):
    tgt_code = device % 2 ** (level_idx + 1)
    return lax.dynamic_slice_in_dim(velocity, tgt_code * tgt_count, tgt_count)


def own_part(current, omegas, my_child, level_idx):
    vec_len = current.shape[-1]
    weights, coord_in, coord_out = level_tables(level_idx % 2)
    coord_mine = jnp.where(my_child == 0, coord_in[0], coord_in[1])
    weight_mine = jnp.where(my_child == 0, weights[:vec_len], weights[vec_len:])
    turned = rotate(current, -omegas[None, :, None] * coord_mine[None, None, :])
    return jnp.dot(
        turned.reshape(-1, vec_len),
        weight_mine,
        precision=lax.Precision.HIGHEST,
        preferred_element_type=jnp.float32,
    )


def far_part(own_term, partner, omegas, my_child, level_idx):
    vec_len = partner.shape[-1]
    weights, coord_in, coord_out = level_tables(level_idx % 2)
    coord_other = jnp.where(my_child == 0, coord_in[1], coord_in[0])
    weight_other = jnp.where(my_child == 0, weights[vec_len:], weights[:vec_len])
    turned = rotate(partner, -omegas[None, :, None] * coord_other[None, None, :])
    far_term = jnp.dot(
        turned.reshape(-1, vec_len),
        weight_other,
        precision=lax.Precision.HIGHEST,
        preferred_element_type=jnp.float32,
    )
    mixture = (own_term + far_term).reshape(partner.shape)
    return rotate(mixture, omegas[None, :, None] * coord_out[None, None, :]) * half_root


def body(box_weights, velocity, switch_kernel):
    box_count = lax.axis_size("box")
    sub_count = lax.axis_size("sub")
    box_bits = box_count.bit_length() - 1
    sub_bits = sub_count.bit_length() - 1
    levels = box_bits + sub_bits
    box_index = lax.axis_index("box")
    sub_index = lax.axis_index("sub")
    device = box_index * sub_count + sub_index
    src_count = box_weights.shape[0]
    tgt_count = box_weights.shape[1]
    vec_len = box_weights.shape[2]
    current = box_weights
    bit_idx = 0
    level_idx = bit_idx
    my_child = sub_index // 2**bit_idx % 2
    omegas = level_omegas(velocity, device, level_idx, tgt_count)
    own_term = own_part(current, omegas, my_child, level_idx)
    partner = swapped(current, "sub", bit_idx)
    current = far_part(own_term, partner, omegas, my_child, level_idx)
    spread = lax.all_to_all(current, "box", split_axis=1, concat_axis=0, tiled=True)
    block_width = tgt_count // box_count
    for bit_idx in range(box_bits):
        level_idx = sub_bits + bit_idx
        weights, coord_in, coord_out = level_tables(level_idx % 2)
        row_count = spread.shape[0]
        col_count = spread.shape[1]
        groups = 2 ** (bit_idx + 1)
        vel_table = velocity[: sub_count * groups * tgt_count].reshape(groups, sub_count, tgt_count)
        omegas = lax.dynamic_slice(
            vel_table, (0, sub_index, box_index * block_width), (groups, 1, block_width)
        )
        omegas = omegas.reshape(2, col_count)
        blocks = spread.reshape(row_count // (2 * src_count), 2, src_count, col_count, vec_len)
        merged = merge_blocks(blocks, omegas, weights, coord_in, coord_out)
        spread = merged.reshape(row_count // 2, 2 * col_count, vec_len)
        if level_idx == levels // 2 - 1:
            spread = apply_switch(spread, switch_kernel)
    current = lax.all_to_all(spread, "box", split_axis=1, concat_axis=1, tiled=True)
    return current


def solution(mesh):
    return jax.shard_map(
        body,
        mesh=mesh,
        in_specs=(P(("shot", "box", "sub"), None, None), P("shot"), P()),
        out_specs=P("shot", ("box", "sub"), None),
        check_vma=False,
    )
```

profile of v0, /device:TPU:0, one launch (start us, length us, event | category | flops | bytes accessed | tf_op | source)
XLA Modules:
  0.0 46.1 jit_solution(10633600639100690880)
XLA Ops:
  0.0 0.5 %collective-permute-start = (f32[2,256,128]{2,1,0:T(8,128)}, f32[2,256,128]{2,1,0:T(8,128)S(1)}, u32[]{:S(2)}, u32[]{:S(2)}) collective-permute-start(f32[2,256,128]{2,1,0:T(8,128)} %param.3), channel_id=1, source_target_pairs={{0,1},{1,0},{2,3},{3,2},{4,5},{5,4},{6,7},{7,6},{8,9},{9,8},{10,11... | collective-permute-start | bytes 786440 | tf_op jit(solution)/shard_map/ppermute | solution.py:13
  0.7 0.7 %copy-done.2 = f32[4096]{0:T(1024)S(1)} copy-done((f32[4096]{0:T(1024)S(1)}, f32[4096]{0:T(1024)}, u32[]{:S(2)}) %copy-start.2) | copy-done | bytes 16408
  1.8 0.2 select_reduce_fusion.2
  2.0 0.3 select_reduce_fusion.1
  2.3 0.1 broadcast_multiply_fusion
  2.5 0.1 mul.1285
  2.6 0.1 mul.1290
  2.8 0.1 mul.1344
  2.9 0.1 mul.1350
  3.2 0.5 %slice-done.1 = f32[2048]{0:T(1024)S(1)} async-done(((f32[4096]{0:T(1024)}), f32[2048]{0:T(1024)S(1)}, s32[]{:S(2)}) %slice-start.1) | async-done | bytes 8216 | tf_op jit(solution)/shard_map/slice | solution.py:155
  3.9 0.3 multiply_cosine_fusion.5
  4.2 0.3 multiply_cosine_fusion.8
  4.6 0.4 slice-done
  5.2 0.3 broadcast_select_fusion
  5.5 0.1 mul.1347
  5.7 0.1 mul.1353
  5.9 0.5 %multiply_cosine_fusion.7 = (f32[2,64,64]{2,1,0:T(8,128)S(1)}, f32[2,64,64]{2,1,0:T(8,128)S(1)}, f32[2,64,64]{2,1,0:T(8,128)S(1)}, f32[2,64,64]{2,1,0:T(8,128)S(1)}) fusion(f32[64]{0:T(128)S(1)} %squeeze_stack_reshape.16, f32[2,64]{1,0:T(2,128)S(1)} %neg.34, f32[64]{0:T(128)S(1)} %squeeze_stack_reshape.17), kind=kLoop, calls=%fused_computation.103 | loop fusion | flops 16384 | bytes 132096 | tf_op jit(solution)/shard_map/cos | solution.py:59
  6.6 1.0 %multiply_cosine_fusion.2 = (f32[256,64]{1,0:T(8,128)S(1)}, f32[256,64]{1,0:T(8,128)S(1)}, f32[256,64]{1,0:T(8,128)S(1)}, f32[256,64]{1,0:T(8,128)S(1)}) fusion(f32[64]{0:T(128)S(1)} %get-tuple-element.97, f32[256]{0:T(256)S(1)} %get-tuple-element.7, f32[64]{0:T(128)S(1)} %get-tuple-element.98), kind=kLoop, calls=%fused_computation.59 | loop fusion | flops 32768 | bytes 263680 | tf_op jit(solution)/shard_map/cos | solution.py:59
  7.6 0.2 multiply_subtract_fusion.9
  7.8 0.1 pad_maximum_fusion
  7.9 0.3 multiply_cosine_fusion.4
  8.2 0.3 multiply_cosine_fusion.11
  8.6 0.1 select_n.114
  8.7 0.1 select_n.117
  8.8 0.1 mul.1391
  8.9 0.1 mul.1392
  9.1 0.4 fusion.39
  9.5 0.2 multiply_subtract_fusion.8
  9.6 0.1 pad_maximum_fusion.1
  9.8 0.4 convolution_add_fusion
  10.1 0.1 fusion.38
  10.3 0.1 copy.42
  10.6 0.8 %copy.29 = f32[2,256,128]{2,0,1:T(2,128)} copy(f32[2,256,128]{1,2,0:T(8,128)S(1)} %maximum_multiply_fusion) | data formatting | bytes 524288 | tf_op jit(solution)/shard_map/mul | solution.py:124
  11.4 6.8 %all-to-all-start = ((f32[2,256,128]{2,0,1:T(2,128)}), f32[2,256,128]{2,0,1:T(2,128)S(1)}, u32[]{:S(2)}, u32[]{:S(2)}) async-start(f32[2,256,128]{2,0,1:T(2,128)} %copy.29), calls=%async_computation | async-start | bytes 524288 | tf_op jit(solution)/shard_map/all_to_all | solution.py:147
  18.2 0.2 multiply_cosine_fusion.9
  18.4 1.0 %multiply_cosine_fusion.1 = (f32[2,128,64]{2,1,0:T(8,128)S(1)}, f32[2,128,64]{2,1,0:T(8,128)S(1)}, f32[2,128,64]{2,1,0:T(8,128)S(1)}, f32[2,128,64]{2,1,0:T(8,128)S(1)}) fusion(f32[64]{0:T(128)S(1)} %mul.1317, f32[2,128]{1,0:T(2,128)S(1)} %neg.35, f32[64]{0:T(128)S(1)} %mul.1330), kind=kLoop, calls=%fused_computation.57 | loop fusion | flops 32768 | bytes 263680 | tf_op jit(solution)/shard_map/cos | solution.py:59
  19.4 8.4 %all-to-all-done = f32[2,256,128]{2,0,1:T(2,128)S(1)} async-done(((f32[2,256,128]{2,0,1:T(2,128)}), f32[2,256,128]{2,0,1:T(2,128)S(1)}, u32[]{:S(2)}, u32[]{:S(2)}) %all-to-all-start) | async-done | bytes 262176 | tf_op jit(solution)/shard_map/all_to_all | solution.py:147
  28.3 0.7 %fusion = f32[4,2,2,32,128]{4,3,2,1,0:T(8,128)S(1)} fusion(f32[4,2,2,32,64]{4,3,2,1,0:T(8,128)S(1)} %get-tuple-element.32, f32[4,2,2,32,64]{4,3,2,1,0:T(8,128)S(1)} %get-tuple-element.31, f32[4,2,2,32,64]{4,3,2,1,0:T(8,128)S(1)} %get-tuple-element.30, f32[4,2,2,32,64]{4,3,2,1,0:T(8,128)S(1)} %get-tuple-element.29, ...), kind=kOutput, calls=%fused_computation.2 | convolution fusion | flops 201719808 | bytes 917504 | tf_op jit(solution)/shard_map/dot_general | solution.py:72
  28.9 0.2 multiply_subtract_fusion.5
  29.1 0.4 fusion.22
  29.9 0.7 %fusion.8 = f32[2,2,2,64,128]{4,3,2,1,0:T(8,128)S(1)} fusion(f32[2,2,2,64,64]{4,3,2,1,0:T(8,128)S(1)} %get-tuple-element.24, f32[2,2,2,64,64]{4,3,2,1,0:T(8,128)S(1)} %get-tuple-element.23, f32[2,2,2,64,64]{4,3,2,1,0:T(8,128)S(1)} %get-tuple-element.22, f32[2,2,2,64,64]{4,3,2,1,0:T(8,128)S(1)} %get-tuple-element.21, f32[128,128]{1,0:T(8,128)S(1)} %mul.1392, ...), kind=kOutput, calls=%fused_computation.10 | convolution fusion | flops 201752576 | bytes 917504 | tf_op jit(solution)/shard_map/dot_general | solution.py:72
  30.6 0.2 multiply_subtract_fusion.2
  30.8 0.1 maximum_multiply_fusion.3
  31.1 0.1 multiply_subtract_fusion
  31.3 0.9 %convolution_bitcast_fusion = f32[1,2,2,128,128]{3,4,2,1,0:T(8,128)S(1)} fusion(f32[1,2,2,128,64]{4,3,2,1,0:T(8,128)S(1)} %get-tuple-element.12, f32[1,2,2,128,64]{4,3,2,1,0:T(8,128)S(1)} %get-tuple-element.11, f32[1,2,2,128,64]{4,3,2,1,0:T(8,128)S(1)} %get-tuple-element.104, f32[1,2,2,128,64]{4,3,2,1,0:T(8,128)S(1)} %get-tuple-element.105, ...), kind=kOutput, calls=%fused_computation | convolution fusion | flops 201719808 | bytes 917504 | tf_op jit(solution)/shard_map/dot_general | solution.py:72
  32.7 0.1 copy.35
  32.8 12.5 %all_to_all.20 = f32[2,256,128]{2,0,1:T(2,128)S(1)} all-to-all(f32[2,256,128]{2,0,1:T(2,128)S(1)} %copy.35), channel_id=1, replica_groups=mesh['shot'=2,'box'=8,'sub'=2] {'box'}, dimensions={1} | all-to-all | bytes 524288 | tf_op jit(solution)/shard_map/all_to_all | solution.py:165
  45.3 0.7 %copy.36 = f32[2,256,128]{2,1,0:T(8,128)} copy(f32[2,256,128]{2,0,1:T(2,128)S(1)} %all_to_all.20) | data formatting | bytes 524288 | tf_op jit(solution)/shard_map/all_to_all | solution.py:165
  (66 shorter events, 3.1 us)
Async XLA Ops:
  0.0 29.1 %copy-start = (f32[128,128]{1,0:T(8,128)S(1)}, f32[128,128]{1,0:T(8,128)}, u32[]{:S(2)}) copy-start(f32[128,128]{1,0:T(8,128)} %param.5) | copy-start | bytes 196612
  0.0 9.4 %collective-permute-start = (f32[2,256,128]{2,1,0:T(8,128)}, f32[2,256,128]{2,1,0:T(8,128)S(1)}, u32[]{:S(2)}, u32[]{:S(2)}) collective-permute-start(f32[2,256,128]{2,1,0:T(8,128)} %param.3), channel_id=1, source_target_pairs={{0,1},{1,0},{2,3},{3,2},{4,5},{5,4},{6,7},{7,6},{8,9},{9,8},{10,11... | collective-permute-start | bytes 786440 | tf_op jit(solution)/shard_map/ppermute | solution.py:13
  0.7 0.7 %copy-start.2 = (f32[4096]{0:T(1024)S(1)}, f32[4096]{0:T(1024)}, u32[]{:S(2)}) copy-start(f32[4096]{0:T(1024)} %param.4) | copy-start | bytes 49156
  3.0 0.7 %slice-start.1 = ((f32[4096]{0:T(1024)}), f32[2048]{0:T(1024)S(1)}, s32[]{:S(2)}) async-start(f32[4096]{0:T(1024)} %param.4), calls=%async_computation.3 | async-start | bytes 16384 | tf_op jit(solution)/shard_map/slice | solution.py:155
  4.2 0.7 %slice-start = ((f32[4096]{0:T(1024)}), f32[1024]{0:T(1024)S(1)}, s32[]{:S(2)}) async-start(f32[4096]{0:T(1024)} %param.4), calls=%async_computation.2 | async-start | bytes 8192 | tf_op jit(solution)/shard_map/slice | solution.py:155
  6.6 1.0 %copy-start.1 = (f32[2,256,128]{2,1,0:T(8,128)S(1)}, f32[2,256,128]{2,1,0:T(8,128)}, u32[]{:S(2)}) copy-start(f32[2,256,128]{2,1,0:T(8,128)} %param.3) | copy-start | bytes 786436
  11.4 16.4 %all-to-all-start = ((f32[2,256,128]{2,0,1:T(2,128)}), f32[2,256,128]{2,0,1:T(2,128)S(1)}, u32[]{:S(2)}, u32[]{:S(2)}) async-start(f32[2,256,128]{2,0,1:T(2,128)} %copy.29), calls=%async_computation | async-start | bytes 524288 | tf_op jit(solution)/shard_map/all_to_all | solution.py:147
where the time goes:
time: 46.4 us; the launch traced here: 46.1 us
  blocking collectives  12.5 us (27%)
  waiting for transfers between devices  8.38 us (18%)
  starting transfers between devices  7.3 us (16%)
  local copies, waits for them, and re-layouts  7.19 us (15%)
  other arithmetic  6.78 us (15%)
  matrix products  3.37 us (7%)
  between operations  0.55 us (1%)
    all_to_all x1, blocking collectives, body(): lax.all_to_all(spread, 'box', split_axis=1, concat_axis=1, tiled=True)  12.5 us
    all_to_all x1, waiting for transfers between devices, body(): lax.all_to_all(current, 'box', split_axis=1, concat_axis=0, tiled=True)  8.38 us
    all_to_all x1, starting transfers between devices, body(): lax.all_to_all(current, 'box', split_axis=1, concat_axis=0, tiled=True)  6.81 us
    cos x8, other arithmetic, rotate(): cosines = jnp.cos(angles)  3.91 us
    dot_general x3, matrix products, merge_blocks(): jnp.dot(joined.reshape(-1, 4 * CHEB * CHEB), weights, precision=lax.Preci...  2.23 us
    sub x11, other arithmetic, rotate(): real_part * cosines - imag_part * sine_vals  1.13 us
    unnamed x9, local copies, waits for them, and re-layouts  0.93 us
    slice x6, local copies, waits for them, and re-layouts, body(): velocity[:sub_count * groups * tgt_count]  0.93 us
  transfers between devices with their start and end apart: 2, of which 1 were waited for; matrix products, arithmetic and copies ran while one was open for 18% of the time, Pallas kernels for 0%

commit v1 on v0

--- a/solution.py
+++ b/solution.py
@@ -5,6 +5,18 @@
 
 CHEB = 8
 half_root = 0.7071067811865476
+
+
+def split_up(value, dim, size):
+    shape = value.shape
+    blocks = value.reshape(*shape[:dim], size, shape[dim] // size, *shape[dim + 1 :])
+    return jnp.moveaxis(blocks, dim, 0)
+
+
+def joined_along(blocks, dim):
+    shape = list(blocks.shape[1:])
+    shape[dim] *= blocks.shape[0]
+    return jnp.moveaxis(blocks, 0, dim).reshape(shape)
 
 
 def swapped(value, axis, apart):
@@ -162,7 +174,14 @@
         spread = merged.reshape(row_count // 2, 2 * col_count, vec_len)
         if level_idx == levels // 2 - 1:
             spread = apply_switch(spread, switch_kernel)
-    current = lax.all_to_all(spread, "box", split_axis=1, concat_axis=1, tiled=True)
+    size, here = (lax.axis_size("box"), lax.axis_index("box"))
+    parts = split_up(spread, 1, size)
+    done = [parts[here]]
+    for step in range(1, size):
+        sent = parts[(here + step) % size]
+        done.append(lax.ppermute(sent, "box", [(i, (i + step) % size) for i in range(size)]))
+    parts = jnp.stack(done)[(here - jnp.arange(size)) % size]
+    current = joined_along(parts, 1)
     return current
 
 

time: 46.4 us -> 47.9 us (1.032)
  blocking collectives: 12.5 us -> 0 us
  starting transfers between devices: 7.3 us -> 17.8 us
  waiting for transfers between devices: 8.38 us -> 10.8 us
  other arithmetic: 6.78 us -> 8.63 us
  local copies, waits for them, and re-layouts: 7.19 us -> 6.22 us
    all_to_all x1 -> x0, blocking collectives: 12.5 us -> none  [body(): lax.all_to_all(spread, 'box', split_axis=1, concat_axis=1, tiled=True)]
    ppermute x0 -> x7, starting transfers between devices: none -> 10.5 us  [body(): lax.ppermute(sent, 'box', [(i, (i + step) % size) for i in range(size)])]
    ppermute x0 -> x7, waiting for transfers between devices: none -> 2.45 us  [body(): lax.ppermute(sent, 'box', [(i, (i + step) % size) for i in range(size)])]
    mul x1, other arithmetic: 0.03 us -> 1.06 us  [far_part(): rotate(mixture, omegas[None, :, None] * coord_out[None, None, :])]
    mul x1 -> x0, local copies, waits for them, and re-layouts: 0.84 us -> none  [far_part(): rotate(mixture, omegas[None, :, None] * coord_out[None, None, :])]
    transpose x0 -> x1, local copies, waits for them, and re-layouts: none -> 0.72 us  [joined_along(): return jnp.moveaxis(blocks, 0, dim).reshape(shape)]
    all_to_all x1 -> x0, local copies, waits for them, and re-layouts: 0.72 us -> none  [body(): lax.all_to_all(spread, 'box', split_axis=1, concat_axis=1, tiled=True)]
    gather x0 -> x1, local copies, waits for them, and re-layouts: none -> 0.56 us  [body(): parts = jnp.stack(done)[(here - jnp.arange(size)) % size]]
  transfers between devices with their start and end apart: 2 -> 9, of which waited for: 1 -> 4; matrix products, arithmetic and copies ran while one was open for 18% -> 18% of each run, Pallas kernels for 0% -> 0%
where the time goes in v1:
time: 47.9 us; the launch traced here: 47.5 us
  starting transfers between devices  17.8 us (37%)
  waiting for transfers between devices  10.8 us (23%)
  other arithmetic  8.63 us (18%)
  local copies, waits for them, and re-layouts  6.22 us (13%)
  matrix products  3.37 us (7%)
  between operations  0.66 us (1%)
    ppermute x7, starting transfers between devices, body(): lax.ppermute(sent, 'box', [(i, (i + step) % size) for i in range(size)])  10.5 us
    all_to_all x1, waiting for transfers between devices, body(): lax.all_to_all(current, 'box', split_axis=1, concat_axis=0, tiled=True)  8.38 us
    all_to_all x1, starting transfers between devices, body(): lax.all_to_all(current, 'box', split_axis=1, concat_axis=0, tiled=True)  6.81 us
    cos x8, other arithmetic, rotate(): cosines = jnp.cos(angles)  4.14 us
    ppermute x7, waiting for transfers between devices, body(): lax.ppermute(sent, 'box', [(i, (i + step) % size) for i in range(size)])  2.45 us
    dot_general x3, matrix products, merge_blocks(): jnp.dot(joined.reshape(-1, 4 * CHEB * CHEB), weights, precision=lax.Preci...  2.22 us
    sub x11, other arithmetic, rotate(): real_part * cosines - imag_part * sine_vals  1.59 us
    mul x1, other arithmetic, far_part(): rotate(mixture, omegas[None, :, None] * coord_out[None, None, :])  1.06 us
  transfers between devices with their start and end apart: 9, of which 4 were waited for; matrix products, arithmetic and copies ran while one was open for 18% of the time, Pallas kernels for 0%

profile of v1, /device:TPU:0, one launch (start us, length us, event | category | flops | bytes accessed | tf_op | source)
XLA Modules:
  0.0 47.5 jit_solution(15765779093555726812)
XLA Ops:
  0.0 0.5 %collective-permute-start = (f32[2,256,128]{2,1,0:T(8,128)}, f32[2,256,128]{2,1,0:T(8,128)S(1)}, u32[]{:S(2)}, u32[]{:S(2)}) collective-permute-start(f32[2,256,128]{2,1,0:T(8,128)} %param.3), channel_id=1, source_target_pairs={{0,1},{1,0},{2,3},{3,2},{4,5},{5,4},{6,7},{7,6},{8,9},{9,8},{10,11... | collective-permute-start | bytes 786440 | tf_op jit(solution)/shard_map/ppermute | solution.py:25
  0.7 0.7 %copy-done.2 = f32[4096]{0:T(1024)S(1)} copy-done((f32[4096]{0:T(1024)S(1)}, f32[4096]{0:T(1024)}, u32[]{:S(2)}) %copy-start.2) | copy-done | bytes 16408
  1.8 0.2 select_reduce_fusion.2
  2.0 0.3 select_reduce_fusion.1
  2.4 0.1 broadcast_multiply_fusion
  3.2 0.5 %slice-done.1 = f32[2048]{0:T(1024)S(1)} async-done(((f32[4096]{0:T(1024)}), f32[2048]{0:T(1024)S(1)}, s32[]{:S(2)}) %slice-start.1) | async-done | bytes 8216 | tf_op jit(solution)/shard_map/slice | solution.py:167
  3.9 0.3 multiply_cosine_fusion.6
  4.3 0.5 %multiply_cosine_fusion.2 = (f32[256,64]{1,0:T(8,128)S(1)}, f32[256,64]{1,0:T(8,128)S(1)}) fusion(f32[64]{0:T(128)S(1)} %mul.1304, f32[256]{0:T(256)S(1)} %get-tuple-element.8), kind=kLoop, calls=%fused_computation.62 | loop fusion | flops 16384 | bytes 132352 | tf_op jit(solution)/shard_map/cos | solution.py:71
  4.8 0.1 slice-done
  5.2 0.3 broadcast_select_fusion
  5.5 0.1 mul.1349
  5.9 0.5 %multiply_cosine_fusion.8 = (f32[2,64,64]{2,1,0:T(8,128)S(1)}, f32[2,64,64]{2,1,0:T(8,128)S(1)}, f32[2,64,64]{2,1,0:T(8,128)S(1)}, f32[2,64,64]{2,1,0:T(8,128)S(1)}) fusion(f32[64]{0:T(128)S(1)} %squeeze_stack_reshape.16, f32[2,64]{1,0:T(2,128)S(1)} %neg.34, f32[64]{0:T(128)S(1)} %squeeze_stack_reshape.17), kind=kLoop, calls=%fused_computation.106 | loop fusion | flops 16384 | bytes 132096 | tf_op jit(solution)/shard_map/cos | solution.py:71
  6.6 1.0 %multiply_cosine_fusion.3 = (f32[256,64]{1,0:T(8,128)S(1)}, f32[256,64]{1,0:T(8,128)S(1)}, f32[256,64]{1,0:T(8,128)S(1)}, f32[256,64]{1,0:T(8,128)S(1)}) fusion(f32[64]{0:T(128)S(1)} %get-tuple-element.104, f32[256]{0:T(256)S(1)} %get-tuple-element.7, f32[64]{0:T(128)S(1)} %get-tuple-element.105), kind=kLoop, calls=%fused_computation.64 | loop fusion | flops 32768 | bytes 263680 | tf_op jit(solution)/shard_map/cos | solution.py:71
  7.6 0.2 multiply_subtract_fusion.10
  7.8 0.1 pad_maximum_fusion
  7.9 0.3 multiply_cosine_fusion.5
  8.2 0.3 multiply_cosine_fusion.11
  8.7 0.1 select_n.189
  9.2 0.4 fusion.42
  9.6 0.2 multiply_subtract_fusion.9
  9.8 0.1 pad_maximum_fusion.1
  9.9 0.4 convolution_add_fusion
  10.4 0.5 %multiply_subtract_fusion.8 = (f32[2,256,64]{2,0,1:T(2,128)S(1)}, f32[2,256,64]{2,0,1:T(2,128)S(1)}) fusion(f32[2,256,64]{2,1,0:T(8,128)S(1)} %get-tuple-element.47, f32[2,256,64]{2,1,0:T(8,128)S(1)} %get-tuple-element.46, f32[256,64]{1,0:T(8,128)S(1)} %get-tuple-element.89, f32[256,64]{1,0:T(8,128)S(1)} %get-tuple-element.88), kind=kLoop, calls=%fused_computation.52 | loop fusion | flops 196608 | bytes 655360 | tf_op jit(solution)/shard_map/sub | solution.py:74
  10.9 1.1 %maximum_multiply_fusion = f32[2,256,128]{2,0,1:T(2,128)} fusion(f32[2,256,64]{2,0,1:T(2,128)S(1)} %get-tuple-element.10, f32[2,256,64]{2,0,1:T(2,128)S(1)} %get-tuple-element.9), kind=kLoop, calls=%fused_computation.28 | loop fusion | flops 131072 | bytes 524288 | tf_op jit(solution)/shard_map/mul | solution.py:136
  12.0 6.8 %all-to-all-start = ((f32[2,256,128]{2,0,1:T(2,128)}), f32[2,256,128]{2,0,1:T(2,128)S(1)}, u32[]{:S(2)}, u32[]{:S(2)}) async-start(f32[2,256,128]{2,0,1:T(2,128)} %maximum_multiply_fusion), calls=%async_computation | async-start | bytes 524288 | tf_op jit(solution)/shard_map/all_to_all | solution.py:159
  18.8 0.2 multiply_cosine_fusion.9
  19.0 1.0 %multiply_cosine_fusion.1 = (f32[2,128,64]{2,1,0:T(8,128)S(1)}, f32[2,128,64]{2,1,0:T(8,128)S(1)}, f32[2,128,64]{2,1,0:T(8,128)S(1)}, f32[2,128,64]{2,1,0:T(8,128)S(1)}) fusion(f32[64]{0:T(128)S(1)} %mul.1319, f32[2,128]{1,0:T(2,128)S(1)} %neg.35, f32[64]{0:T(128)S(1)} %mul.1332), kind=kLoop, calls=%fused_computation.60 | loop fusion | flops 32768 | bytes 263680 | tf_op jit(solution)/shard_map/cos | solution.py:71
  20.0 8.4 %all-to-all-done = f32[2,256,128]{2,0,1:T(2,128)S(1)} async-done(((f32[2,256,128]{2,0,1:T(2,128)}), f32[2,256,128]{2,0,1:T(2,128)S(1)}, u32[]{:S(2)}, u32[]{:S(2)}) %all-to-all-start) | async-done | bytes 262176 | tf_op jit(solution)/shard_map/all_to_all | solution.py:159
  28.8 0.7 %fusion = f32[4,2,2,32,128]{4,3,2,1,0:T(8,128)S(1)} fusion(f32[4,2,2,32,64]{4,3,2,1,0:T(8,128)S(1)} %get-tuple-element.32, f32[4,2,2,32,64]{4,3,2,1,0:T(8,128)S(1)} %get-tuple-element.31, f32[4,2,2,32,64]{4,3,2,1,0:T(8,128)S(1)} %get-tuple-element.30, f32[4,2,2,32,64]{4,3,2,1,0:T(8,128)S(1)} %get-tuple-element.29, ...), kind=kOutput, calls=%fused_computation.3 | convolution fusion | flops 201719808 | bytes 917504 | tf_op jit(solution)/shard_map/dot_general | solution.py:84
  29.5 0.2 multiply_subtract_fusion.5
  29.6 0.4 fusion.22
  30.5 0.7 %fusion.8 = f32[2,2,2,64,128]{4,3,2,1,0:T(8,128)S(1)} fusion(f32[2,2,2,64,64]{4,3,2,1,0:T(8,128)S(1)} %get-tuple-element.26, f32[2,2,2,64,64]{4,3,2,1,0:T(8,128)S(1)} %get-tuple-element.25, f32[2,2,2,64,64]{4,3,2,1,0:T(8,128)S(1)} %get-tuple-element.24, f32[2,2,2,64,64]{4,3,2,1,0:T(8,128)S(1)} %get-tuple-element.23, f32[128,128]{1,0:T(8,128)S(1)} %mul.1394, ...), kind=kOutput, calls=%fused_computation.11 | convolution fusion | flops 201752576 | bytes 917504 | tf_op jit(solution)/shard_map/dot_general | solution.py:84
  31.1 0.2 multiply_subtract_fusion.2
  31.3 0.1 maximum_multiply_fusion.3
  31.7 0.1 multiply_subtract_fusion
  31.8 0.9 %convolution_bitcast_fusion = f32[1,2,2,128,128]{3,4,2,1,0:T(8,128)S(1)} fusion(f32[1,2,2,128,64]{4,3,2,1,0:T(8,128)S(1)} %get-tuple-element.14, f32[1,2,2,128,64]{4,3,2,1,0:T(8,128)S(1)} %get-tuple-element.13, f32[1,2,2,128,64]{4,3,2,1,0:T(8,128)S(1)} %get-tuple-element.111, f32[1,2,2,128,64]{4,3,2,1,0:T(8,128)S(1)} %get-tuple-element.112, ...), kind=kOutput, calls=%fused_computation.1 | convolution fusion | flops 201719808 | bytes 917504 | tf_op jit(solution)/shard_map/dot_general | solution.py:84
  33.0 0.1 maximum_multiply_fusion.4
  33.2 1.5 %collective-permute-start.1 = (f32[2,32,128]{2,1,0:T(8,128)S(1)}, f32[2,32,128]{2,1,0:T(8,128)S(1)}, u32[]{:S(2)}, u32[]{:S(2)}) collective-permute-start(f32[2,32,128]{2,1,0:T(8,128)S(1)} %get-tuple-element.39), channel_id=1, source_target_pairs={{0,2},{2,4},{4,6},{6,8},{8,10},{10,12},{12,14},{14,0},{1,3},{3,5},... | collective-permute-start | bytes 98312 | tf_op jit(solution)/shard_map/ppermute | solution.py:182
  34.7 1.7 %collective-permute-start.3 = (f32[2,32,128]{2,1,0:T(8,128)S(1)}, f32[2,32,128]{2,1,0:T(8,128)S(1)}, u32[]{:S(2)}, u32[]{:S(2)}) collective-permute-start(f32[2,32,128]{2,1,0:T(8,128)S(1)} %get-tuple-element.37), channel_id=1, source_target_pairs={{0,6},{2,8},{4,10},{6,12},{8,14},{10,0},{12,2},{14,4},{1,7},{3,9},... | collective-permute-start | bytes 98312 | tf_op jit(solution)/shard_map/ppermute | solution.py:182
  36.4 3.2 %collective-permute-start.4 = (f32[2,32,128]{2,1,0:T(8,128)S(1)}, f32[2,32,128]{2,1,0:T(8,128)S(1)}, u32[]{:S(2)}, u32[]{:S(2)}) collective-permute-start(f32[2,32,128]{2,1,0:T(8,128)S(1)} %get-tuple-element.36), channel_id=1, source_target_pairs={{0,8},{2,10},{4,12},{6,14},{8,0},{10,2},{12,4},{14,6},{1,9},{3,11}... | collective-permute-start | bytes 98312 | tf_op jit(solution)/shard_map/ppermute | solution.py:182
  39.6 0.9 %collective-permute-start.5 = (f32[2,32,128]{2,1,0:T(8,128)S(1)}, f32[2,32,128]{2,1,0:T(8,128)S(1)}, u32[]{:S(2)}, u32[]{:S(2)}) collective-permute-start(f32[2,32,128]{2,1,0:T(8,128)S(1)} %get-tuple-element.35), channel_id=1, source_target_pairs={{0,10},{2,12},{4,14},{6,0},{8,2},{10,4},{12,6},{14,8},{1,11},{3,13... | collective-permute-start | bytes 98312 | tf_op jit(solution)/shard_map/ppermute | solution.py:182
  40.5 1.8 %collective-permute-start.6 = (f32[2,32,128]{2,1,0:T(8,128)S(1)}, f32[2,32,128]{2,1,0:T(8,128)S(1)}, u32[]{:S(2)}, u32[]{:S(2)}) collective-permute-start(f32[2,32,128]{2,1,0:T(8,128)S(1)} %get-tuple-element.34), channel_id=1, source_target_pairs={{0,12},{2,14},{4,0},{6,2},{8,4},{10,6},{12,8},{14,10},{1,13},{3,15... | collective-permute-start | bytes 98312 | tf_op jit(solution)/shard_map/ppermute | solution.py:182
  42.3 1.4 %collective-permute-start.7 = (f32[2,32,128]{2,1,0:T(8,128)S(1)}, f32[2,32,128]{2,1,0:T(8,128)S(1)}, u32[]{:S(2)}, u32[]{:S(2)}) collective-permute-start(f32[2,32,128]{2,1,0:T(8,128)S(1)} %get-tuple-element.33), channel_id=1, source_target_pairs={{0,14},{2,0},{4,2},{6,4},{8,6},{10,8},{12,10},{14,12},{1,15},{3,1}... | collective-permute-start | bytes 98312 | tf_op jit(solution)/shard_map/ppermute | solution.py:182
  43.8 0.6 %collective-permute-done.5 = f32[2,32,128]{2,1,0:T(8,128)S(1)} collective-permute-done((f32[2,32,128]{2,1,0:T(8,128)S(1)}, f32[2,32,128]{2,1,0:T(8,128)S(1)}, u32[]{:S(2)}, u32[]{:S(2)}) %collective-permute-start.5) | collective-permute-done | bytes 32800 | tf_op jit(solution)/shard_map/ppermute | solution.py:182
  44.4 0.4 collective-permute-done.6
  44.8 1.5 %collective-permute-done.7 = f32[2,32,128]{2,1,0:T(8,128)S(1)} collective-permute-done((f32[2,32,128]{2,1,0:T(8,128)S(1)}, f32[2,32,128]{2,1,0:T(8,128)S(1)}, u32[]{:S(2)}, u32[]{:S(2)}) %collective-permute-start.7) | collective-permute-done | bytes 32800 | tf_op jit(solution)/shard_map/ppermute | solution.py:182
  46.3 0.6 %gather_fusion = f32[8,2,32,128]{3,2,1,0:T(8,128)S(1)} fusion(f32[8,2,32,128]{3,2,1,0:T(8,128)S(1)} %bitcast_dynamic-update-slice_fusion, s32[1024]{0:T(1024)S(1)} %pad_clamp_fusion), kind=kCustom, calls=%fused_computation | custom fusion | bytes 524320 | tf_op jit(solution)/shard_map/gather | solution.py:183
  46.8 0.7 %copy.28 = f32[2,8,32,128]{3,2,1,0:T(8,128)} copy(f32[2,8,32,128]{3,2,0,1:T(8,128)S(1)} %bitcast.126) | data formatting | bytes 524288 | tf_op jit(solution)/shard_map/transpose | solution.py:19
  (85 shorter events, 4.0 us)
Async XLA Ops:
  0.0 29.6 %copy-start = (f32[128,128]{1,0:T(8,128)S(1)}, f32[128,128]{1,0:T(8,128)}, u32[]{:S(2)}) copy-start(f32[128,128]{1,0:T(8,128)} %param.5) | copy-start | bytes 196612
  0.0 9.6 %collective-permute-start = (f32[2,256,128]{2,1,0:T(8,128)}, f32[2,256,128]{2,1,0:T(8,128)S(1)}, u32[]{:S(2)}, u32[]{:S(2)}) collective-permute-start(f32[2,256,128]{2,1,0:T(8,128)} %param.3), channel_id=1, source_target_pairs={{0,1},{1,0},{2,3},{3,2},{4,5},{5,4},{6,7},{7,6},{8,9},{9,8},{10,11... | collective-permute-start | bytes 786440 | tf_op jit(solution)/shard_map/ppermute | solution.py:25
  0.7 0.7 %copy-start.2 = (f32[4096]{0:T(1024)S(1)}, f32[4096]{0:T(1024)}, u32[]{:S(2)}) copy-start(f32[4096]{0:T(1024)} %param.4) | copy-start | bytes 49156
  3.0 0.7 %slice-start.1 = ((f32[4096]{0:T(1024)}), f32[2048]{0:T(1024)S(1)}, s32[]{:S(2)}) async-start(f32[4096]{0:T(1024)} %param.4), calls=%async_computation.2 | async-start | bytes 16384 | tf_op jit(solution)/shard_map/slice | solution.py:167
  4.2 0.7 %slice-start = ((f32[4096]{0:T(1024)}), f32[1024]{0:T(1024)S(1)}, s32[]{:S(2)}) async-start(f32[4096]{0:T(1024)} %param.4), calls=%async_computation.1 | async-start | bytes 8192 | tf_op jit(solution)/shard_map/slice | solution.py:167
  6.6 1.0 %copy-start.1 = (f32[2,256,128]{2,1,0:T(8,128)S(1)}, f32[2,256,128]{2,1,0:T(8,128)}, u32[]{:S(2)}) copy-start(f32[2,256,128]{2,1,0:T(8,128)} %param.3) | copy-start | bytes 786436
  12.0 16.4 %all-to-all-start = ((f32[2,256,128]{2,0,1:T(2,128)}), f32[2,256,128]{2,0,1:T(2,128)S(1)}, u32[]{:S(2)}, u32[]{:S(2)}) async-start(f32[2,256,128]{2,0,1:T(2,128)} %maximum_multiply_fusion), calls=%async_computation | async-start | bytes 524288 | tf_op jit(solution)/shard_map/all_to_all | solution.py:159
  33.2 7.3 %collective-permute-start.1 = (f32[2,32,128]{2,1,0:T(8,128)S(1)}, f32[2,32,128]{2,1,0:T(8,128)S(1)}, u32[]{:S(2)}, u32[]{:S(2)}) collective-permute-start(f32[2,32,128]{2,1,0:T(8,128)S(1)} %get-tuple-element.39), channel_id=1, source_target_pairs={{0,2},{2,4},{4,6},{6,8},{8,10},{10,12},{12,14},{14,0},{1,3},{3,5},... | collective-permute-start | bytes 98312 | tf_op jit(solution)/shard_map/ppermute | solution.py:182
  34.7 7.7 %collective-permute-start.2 = (f32[2,32,128]{2,1,0:T(8,128)S(1)}, f32[2,32,128]{2,1,0:T(8,128)S(1)}, u32[]{:S(2)}, u32[]{:S(2)}) collective-permute-start(f32[2,32,128]{2,1,0:T(8,128)S(1)} %get-tuple-element.38), channel_id=1, source_target_pairs={{0,4},{2,6},{4,8},{6,10},{8,12},{10,14},{12,0},{14,2},{1,5},{3,7},... | collective-permute-start | bytes 98312 | tf_op jit(solution)/shard_map/ppermute | solution.py:182
  34.7 9.0 %collective-permute-start.3 = (f32[2,32,128]{2,1,0:T(8,128)S(1)}, f32[2,32,128]{2,1,0:T(8,128)S(1)}, u32[]{:S(2)}, u32[]{:S(2)}) collective-permute-start(f32[2,32,128]{2,1,0:T(8,128)S(1)} %get-tuple-element.37), channel_id=1, source_target_pairs={{0,6},{2,8},{4,10},{6,12},{8,14},{10,0},{12,2},{14,4},{1,7},{3,9},... | collective-permute-start | bytes 98312 | tf_op jit(solution)/shard_map/ppermute | solution.py:182
  36.4 7.4 %collective-permute-start.4 = (f32[2,32,128]{2,1,0:T(8,128)S(1)}, f32[2,32,128]{2,1,0:T(8,128)S(1)}, u32[]{:S(2)}, u32[]{:S(2)}) collective-permute-start(f32[2,32,128]{2,1,0:T(8,128)S(1)} %get-tuple-element.36), channel_id=1, source_target_pairs={{0,8},{2,10},{4,12},{6,14},{8,0},{10,2},{12,4},{14,6},{1,9},{3,11}... | collective-permute-start | bytes 98312 | tf_op jit(solution)/shard_map/ppermute | solution.py:182
  39.6 4.8 %collective-permute-start.5 = (f32[2,32,128]{2,1,0:T(8,128)S(1)}, f32[2,32,128]{2,1,0:T(8,128)S(1)}, u32[]{:S(2)}, u32[]{:S(2)}) collective-permute-start(f32[2,32,128]{2,1,0:T(8,128)S(1)} %get-tuple-element.35), channel_id=1, source_target_pairs={{0,10},{2,12},{4,14},{6,0},{8,2},{10,4},{12,6},{14,8},{1,11},{3,13... | collective-permute-start | bytes 98312 | tf_op jit(solution)/shard_map/ppermute | solution.py:182
  40.5 4.3 %collective-permute-start.6 = (f32[2,32,128]{2,1,0:T(8,128)S(1)}, f32[2,32,128]{2,1,0:T(8,128)S(1)}, u32[]{:S(2)}, u32[]{:S(2)}) collective-permute-start(f32[2,32,128]{2,1,0:T(8,128)S(1)} %get-tuple-element.34), channel_id=1, source_target_pairs={{0,12},{2,14},{4,0},{6,2},{8,4},{10,6},{12,8},{14,10},{1,13},{3,15... | collective-permute-start | bytes 98312 | tf_op jit(solution)/shard_map/ppermute | solution.py:182
  42.3 3.9 %collective-permute-start.7 = (f32[2,32,128]{2,1,0:T(8,128)S(1)}, f32[2,32,128]{2,1,0:T(8,128)S(1)}, u32[]{:S(2)}, u32[]{:S(2)}) collective-permute-start(f32[2,32,128]{2,1,0:T(8,128)S(1)} %get-tuple-element.33), channel_id=1, source_target_pairs={{0,14},{2,0},{4,2},{6,4},{8,6},{10,8},{12,10},{14,12},{1,15},{3,1}... | collective-permute-start | bytes 98312 | tf_op jit(solution)/shard_map/ppermute | solution.py:182
